TPU v7x, 32 devices: a whole 2x2x4 slice. The times are simulated.
32 devices in a mesh: dp: 8 (over z, core), resp: 4 (over y, x).
Axes of the slice: x: 2, y: 2, z: 4, core: 2. Of those that a mesh axis runs over, the one named last changes fastest.
Arguments:
- queries: bfloat16 [8, 4, 128, 4096], P('dp', 'resp'), may hold values from -6 to 6
- prefix_kv: bfloat16 [8, 256, 1024], P('dp', 'resp'), may hold values from -6 to 6
- resp_kv: bfloat16 [8, 4, 128, 1024], P('dp', 'resp'), may hold values from -6 to 6
- direction: bfloat16 [8, 4, 128, 4096], P('dp', 'resp'), may hold values from -0.09375 to 0.09375
- base_logprob: float32 [8, 4, 128], P('dp', 'resp'), may hold values from -2 to 2
- rollout_logprob: float32 [8, 4, 128], P('dp', 'resp'), may hold values from -2 to 2
- destination: int32 [8, 4, 128], P('dp', 'resp'), may hold values from 0 to 1023, as said below
- advantage: float32 [8, 4], P('dp', 'resp'), may hold values from -4 to 4
- lengths: int32 [8, 4], P('dp', 'resp'), may hold values from 1 to 128, 384 in all within a row
- prefix_blocks: int32 [8, 4], P('dp', 'resp'), may hold values from 1 to 2, as said below
Outputs:
- query_grad: bfloat16 [8, 4, 128, 4096], P('dp', 'resp')
- resp_grad: bfloat16 [8, 4, 128, 1024], P('dp', 'resp')
- prefix_grad: bfloat16 [8, 256, 1024], P('dp', 'resp')
Inputs may be any that keep to these rules, and one draw needn't show every extreme that they name: For each response index r, destination maps the 1024 rollout rows one to one onto the trainer rows; value g * 128 + t names token t of prompt group g; every index of dp holds exactly 16 rows bound for each prompt group. Each response sees the leading prefix_blocks blocks of 128 prompt rows; in every prompt group some response sees all 2. In every prompt group the lengths sum to 384 and one response has 128.
All inputs are finite; a program needn't handle non-finite values.
Results may differ from a plain program's by a relative error of at most 0.011.
Values may be sent and summed in bfloat16 or wider, within the bound.
A program may use at most 128 MiB of HBM per device.

v0:
```python
import math

import jax
import jax.numpy as jnp
from jax import lax
from jax.sharding import PartitionSpec as P

QH = 32
KVH = 4
HD = 128
GQ = 8
BLOCK = 128


loss_scale = 65536.0
clip_lower = 0.8
clip_upper = 1.28


def split_heads(keys_values):
    total_keys = keys_values.shape[0]
    key_heads = keys_values[:, : KVH * HD].reshape(total_keys, KVH, HD).transpose(1, 0, 2)
    value_heads = keys_values[:, KVH * HD :].reshape(total_keys, KVH, HD).transpose(1, 0, 2)
    return (key_heads, value_heads)


def body(
    queries,
    prefix_kv,
    resp_kv,
    direction,
    base_logprob,
    rollout_logprob,
    destination,
    advantage,
    lengths,
    prefix_blocks,
):
    tok_rows = queries.shape[2]
    score_scale = 1.0 / math.sqrt(HD)
    dp_count = lax.axis_size("dp")
    per_peer = tok_rows // dp_count
    targets = destination[0, 0] // tok_rows
    ordering = jnp.argsort(targets, stable=True)
    sent_logprob = rollout_logprob[0, 0][ordering].reshape(dp_count, per_peer)
    sent_slot = (destination[0, 0] % tok_rows)[ordering].reshape(dp_count, per_peer)
    got_logprob, got_slot = (
        lax.all_to_all(sent_logprob, "dp", split_axis=0, concat_axis=0, tiled=True),
        lax.all_to_all(sent_slot, "dp", split_axis=0, concat_axis=0, tiled=True),
    )
    old_rows = (
        jnp.zeros((tok_rows,), jnp.float32).at[got_slot.reshape(-1)].set(got_logprob.reshape(-1))
    )
    prefix_all = lax.all_gather(prefix_kv[0], "resp", axis=0, tiled=True)
    prefix_rows = prefix_all.shape[0]
    total_keys = prefix_rows + tok_rows
    own_kv = resp_kv[0, 0]
    key_heads, value_heads = split_heads(jnp.concatenate([prefix_all, own_kv], axis=0))
    key_index = jnp.arange(total_keys, dtype=jnp.int32)
    query_index = jnp.arange(tok_rows, dtype=jnp.int32)
    in_prefix = (key_index < prefix_rows) & (key_index // BLOCK < prefix_blocks[0, 0])
    in_response = (key_index[None, :] >= prefix_rows) & (
        key_index[None, :] - prefix_rows <= query_index[:, None]
    )
    allowed = in_prefix[None, :] | in_response
    query_heads = queries[0, 0].reshape(tok_rows, KVH, GQ, HD).transpose(1, 0, 2, 3)

    def head_forward(head_inputs):
        query_head, key_head, value_head = head_inputs
        scores = (
            jnp.einsum("rgd,ld->grl", query_head, key_head, preferred_element_type=jnp.float32)
            * score_scale
        )
        scores = jnp.where(allowed[None], scores, -1e30)
        shifted = jnp.exp(scores - jnp.max(scores, axis=-1, keepdims=True))
        prob_bf16 = (shifted / jnp.sum(shifted, axis=-1, keepdims=True)).astype(jnp.bfloat16)
        head_out = jnp.einsum(
            "grl,ld->rgd", prob_bf16, value_head, preferred_element_type=jnp.float32
        )
        return (prob_bf16, head_out)

    prob_all, out_all = lax.map(head_forward, (query_heads, key_heads, value_heads))
    attn_out = out_all.transpose(1, 0, 2, 3).reshape(tok_rows, QH * HD)
    out_bf16 = attn_out.astype(jnp.bfloat16)
    direction_rows = direction[0, 0]
    new_logprob = base_logprob[0, 0] + jnp.einsum(
        "rj,rj->r", out_bf16, direction_rows, preferred_element_type=jnp.float32
    )
    ratio_weight = jnp.clip(jnp.exp(new_logprob - old_rows), clip_lower, clip_upper)
    length_one = lengths[0, 0]
    loss_coeff = jnp.where(
        query_index < length_one,
        -loss_scale * ratio_weight * advantage[0, 0] / length_one.astype(jnp.float32),
        0.0,
    )
    grad_out = (loss_coeff[:, None] * direction_rows.astype(jnp.float32)).astype(jnp.bfloat16)
    grad_heads = grad_out.reshape(tok_rows, KVH, GQ, HD).transpose(1, 0, 2, 3)

    def head_backward(head_inputs):
        key_head, value_head, prob_bf16, head_out, grad_head = head_inputs
        prob_grad = jnp.einsum(
            "rgd,ld->grl", grad_head, value_head, preferred_element_type=jnp.float32
        )
        row_delta = jnp.sum(grad_head.astype(jnp.float32) * head_out, axis=-1).T
        dscore = (
            prob_bf16.astype(jnp.float32) * (prob_grad - row_delta[..., None]) * score_scale
        ).astype(jnp.bfloat16)
        query_part = jnp.einsum("grl,ld->rgd", dscore, key_head, preferred_element_type=jnp.float32)
        return (query_part, dscore)

    query_parts, dscore_all = lax.map(
        head_backward, (key_heads, value_heads, prob_all, out_all, grad_heads)
    )
    query_grad = query_parts.transpose(1, 0, 2, 3).reshape(tok_rows, QH * HD).astype(jnp.bfloat16)
    key_part = jnp.einsum(
        "hgrl,hrgd->lhd", dscore_all, query_heads, preferred_element_type=jnp.float32
    )
    value_part = jnp.einsum(
        "hgrl,hrgd->lhd", prob_all, grad_heads, preferred_element_type=jnp.float32
    )
    kv_grad = jnp.concatenate(
        [key_part.reshape(total_keys, KVH * HD), value_part.reshape(total_keys, KVH * HD)], axis=1
    )
    summed = lax.psum_scatter(kv_grad[:prefix_rows], "resp", scatter_dimension=0, tiled=True)
    resp_part = kv_grad[prefix_rows:]
    return (
        query_grad[None, None],
        resp_part.astype(jnp.bfloat16)[None, None],
        summed.astype(jnp.bfloat16)[None],
    )


def solution(mesh):
    return jax.shard_map(
        body,
        mesh=mesh,
        in_specs=(
            P("dp", "resp", None, None),
            P("dp", "resp", None),
            P("dp", "resp", None, None),
            P("dp", "resp", None, None),
            P("dp", "resp", None),
            P("dp", "resp", None),
            P("dp", "resp", None),
            P("dp", "resp"),
            P("dp", "resp"),
            P("dp", "resp"),
        ),
        out_specs=(P("dp", "resp", None, None), P("dp", "resp", None, None), P("dp", "resp", None)),
        check_vma=False,
    )
```

profile of v0, /device:TPU:0, one launch (start us, length us, event | category | flops | bytes accessed | tf_op | source)
XLA Modules:
  0.0 153.7 jit_solution(10298874838395375511)
XLA Ops:
  8.0 2.5 %sort.17 = (s32[128]{0:T(128)}, s32[128]{0:T(128)S(1)}) sort(s32[128]{0:T(128)S(1)} %get-tuple-element.195, s32[128]{0:T(128)S(1)} %iota.29), dimensions={0}, to_apply=%region_4.5 | sort | flops 896 | bytes 2048 | tf_op jit(solution)/shard_map/jit(argsort)/sort | solution.py:44
  10.5 1.2 gather_fusion
  12.4 6.3 %all-to-all-start = ((s32[8,1,16]{2,1,0:T(1,128)}), s32[8,1,16]{2,1,0:T(1,128)S(1)}, u32[]{:S(2)}, u32[]{:S(2)}) async-start(s32[8,1,16]{2,1,0:T(1,128)} %bitcast.29), calls=%async_computation | async-start | bytes 8192 | tf_op jit(solution)/shard_map/all_to_all | solution.py:49
  18.8 11.5 %all-gather = bf16[1,256,1024]{2,1,0:T(8,128)(2,1)S(1)} all-gather(bf16[1,64,1024]{2,1,0:T(8,128)(2,1)} %param.15), channel_id=2, replica_groups=mesh['dp'=8,'resp'=4] {'resp'}, dimensions={1}, use_global_device_ids=true | all-gather | bytes 655360 | tf_op jit(solution)/shard_map/all_gather | solution.py:54
  32.9 2.4 %broadcast.103.clone = bf16[4,8,128,384]{2,3,1,0:T(8,128)(2,1)} broadcast(bf16[]{:T(256)} %constant.89.clone.1), dimensions={} | broadcast | bytes 3145730 | tf_op jit(solution)/shard_map/broadcast.12
  35.3 15.7 %while.28 = (s32[]{:T(128)}, bf16[4,8,128,384]{2,3,1,0:T(8,128)(2,1)}, f32[4,128,8,128]{1,3,2,0:T(8,128)}, bf16[4,384,128]{1,2,0:T(8,128)(2,1)S(1)}, bf16[4,128,...) while((s32[]{:T(128)}, ...), condition=%wide.region_3.4_spmd.clone.clone, body=%wide.region_0.0_spmd.clone.sunk.clone | while | flops 306464512 | bytes 5444501 | solution.py:82
  36.4 1.0 bitcast_dynamic-update-slice_fusion.7
  37.5 1.7 %fusion.113 = f32[4,128,8,128]{1,3,2,0:T(8,128)} fusion(f32[4,128,8,128]{1,3,2,0:T(8,128)} %get-tuple-element.364, s32[]{:T(128)} %get-tuple-element.362, bf16[4,384,128]{1,2,0:T(8,128)(2,1)S(1)} %get-tuple-element.376, f32[8,128]{1,0:T(8,128)S(1)} %get-tuple-element.342, pred[128,384]{0,1:T(8,128)(4,1)S(1)} %fusion.111, ...), kind=kOutput, calls=%fused_computation.28.clone.1.clone | convolution fusion | flops 203294080 | bytes 1038336 | tf_op jit(solution)/shard_map/while/body/eval_jaxpr/grl,ld->rgd/dot_general | solution.py:77
  40.4 1.0 bitcast_dynamic-update-slice_fusion.7
  41.4 1.8 %fusion.113 = f32[4,128,8,128]{1,3,2,0:T(8,128)} fusion(f32[4,128,8,128]{1,3,2,0:T(8,128)} %get-tuple-element.364, s32[]{:T(128)} %get-tuple-element.362, bf16[4,384,128]{1,2,0:T(8,128)(2,1)S(1)} %get-tuple-element.376, f32[8,128]{1,0:T(8,128)S(1)} %get-tuple-element.342, pred[128,384]{0,1:T(8,128)(4,1)S(1)} %fusion.111, ...), kind=kOutput, calls=%fused_computation.28.clone.1.clone | convolution fusion | flops 203294080 | bytes 1038336 | tf_op jit(solution)/shard_map/while/body/eval_jaxpr/grl,ld->rgd/dot_general | solution.py:77
  44.3 1.0 bitcast_dynamic-update-slice_fusion.7
  45.3 1.7 %fusion.113 = f32[4,128,8,128]{1,3,2,0:T(8,128)} fusion(f32[4,128,8,128]{1,3,2,0:T(8,128)} %get-tuple-element.364, s32[]{:T(128)} %get-tuple-element.362, bf16[4,384,128]{1,2,0:T(8,128)(2,1)S(1)} %get-tuple-element.376, f32[8,128]{1,0:T(8,128)S(1)} %get-tuple-element.342, pred[128,384]{0,1:T(8,128)(4,1)S(1)} %fusion.111, ...), kind=kOutput, calls=%fused_computation.28.clone.1.clone | convolution fusion | flops 203294080 | bytes 1038336 | tf_op jit(solution)/shard_map/while/body/eval_jaxpr/grl,ld->rgd/dot_general | solution.py:77
  48.2 1.1 bitcast_dynamic-update-slice_fusion.7
  49.3 1.7 %fusion.113 = f32[4,128,8,128]{1,3,2,0:T(8,128)} fusion(f32[4,128,8,128]{1,3,2,0:T(8,128)} %get-tuple-element.364, s32[]{:T(128)} %get-tuple-element.362, bf16[4,384,128]{1,2,0:T(8,128)(2,1)S(1)} %get-tuple-element.376, f32[8,128]{1,0:T(8,128)S(1)} %get-tuple-element.342, pred[128,384]{0,1:T(8,128)(4,1)S(1)} %fusion.111, ...), kind=kOutput, calls=%fused_computation.28.clone.1.clone | convolution fusion | flops 203294080 | bytes 1038336 | tf_op jit(solution)/shard_map/while/body/eval_jaxpr/grl,ld->rgd/dot_general | solution.py:77
  51.0 1.1 copy-done.4
  52.1 3.1 %bitcast_convert_fusion = f32[128,4096]{0,1:T(8,128)} fusion(f32[4,128,8,128]{1,3,2,0:T(8,128)} %get-tuple-element.387), kind=kLoop, calls=%fused_computation.54 | loop fusion | flops 1048576 | bytes 4194304
  55.2 2.0 %copy.65 = f32[128,4096]{1,0:T(8,128)S(1)} copy(f32[128,4096]{0,1:T(8,128)} %bitcast_convert_fusion) | data formatting | bytes 4194304
  58.1 1.2 broadcast_convert_fusion
  59.3 2.4 %copy.51 = bf16[1,1,128,4096]{2,3,1,0:T(8,128)(2,1)} copy(bf16[1,1,128,4096]{3,2,1,0:T(8,128)(2,1)} %param.17) | data formatting | bytes 2097152 | tf_op args[3]
  61.7 1.3 gather_fusion.1
  65.1 4.5 %all-to-all-start.1 = ((f32[8,1,16]{2,1,0:T(1,128)}), f32[8,1,16]{2,1,0:T(1,128)S(1)}, u32[]{:S(2)}, u32[]{:S(2)}) async-start(f32[8,1,16]{2,1,0:T(1,128)} %bitcast.32), calls=%async_computation.1 | async-start | bytes 8192 | tf_op jit(solution)/shard_map/all_to_all | solution.py:48
  71.4 3.7 %all-to-all-done.1 = f32[8,1,16]{2,1,0:T(1,128)S(1)} async-done(((f32[8,1,16]{2,1,0:T(1,128)}), f32[8,1,16]{2,1,0:T(1,128)S(1)}, u32[]{:S(2)}, u32[]{:S(2)}) %all-to-all-start.1) | async-done | bytes 544 | tf_op jit(solution)/shard_map/all_to_all | solution.py:48
  76.3 1.1 scatter_custom_fusion
  78.1 1.5 fusion.51
  79.6 1.9 %fusion.72 = f32[4,128,384,1]{2,1,3,0:T(8,128)} fusion(bf16[4,128,8,128]{1,3,2,0:T(8,128)(2,1)S(1)} %fusion.51, bf16[4,8,128,384]{2,3,1,0:T(8,128)(2,1)S(1)} %copy-done.1), kind=kOutput, calls=%fused_computation.94 | convolution fusion | flops 402653184 | bytes 4980736 | tf_op jit(solution)/shard_map/hgrl,hrgd->lhd/dot_general | solution.py:118
  81.5 2.4 %broadcast.103 = bf16[4,8,128,384]{2,3,1,0:T(8,128)(2,1)} broadcast(bf16[]{:T(256)} %constant.89.clone.1), dimensions={} | broadcast | bytes 3145730 | tf_op jit(solution)/shard_map/broadcast.12
  83.9 30.5 %while.27 = (s32[]{:T(128)}, bf16[4,128,8,128]{1,3,2,0:T(8,128)(2,1)}, bf16[4,8,128,384]{2,3,1,0:T(8,128)(2,1)}, bf16[4,384,128]{1,2,0:T(8,128)(2,1)}, bf16[4,8,...) while((s32[]{:T(128)}, ...), condition=%wide.region_8.9_spmd.clone, body=%wide.region_6.8_spmd.sunk.clone | while | flops 203684864 | bytes 29043384 | solution.py:111
  83.9 1.0 constant_dynamic-slice_fusion.8
  85.1 1.1 constant_dynamic-slice_fusion.7
  86.6 2.7 %bitcast_dynamic-update-slice_fusion.6 = (bf16[4,8,128,384]{2,3,1,0:T(8,128)(2,1)}, bf16[8,128,384]{1,2,0:T(8,128)(2,1)S(1)}) fusion(bf16[4,8,128,384]{2,3,1,0:T(8,128)(2,1)} %get-tuple-element.390, s32[]{:T(128)} %get-tuple-element.388, f32[8,128]{1,0:T(8,128)S(1)} %bitcast.236, bf16[4,128,8,128]{1,3,2,0:T(8,128)(2,1)} %get-tuple-element.402, ...), kind=kOutput, calls=%fused_computation.10.clone.1.clone | convolution fusion | flops 102629376 | bytes 2725376 | tf_op jit(solution)/shard_map/while/body/eval_jaxpr/rgd,ld->grl/dot_general | solution.py:101
  89.3 1.2 fusion.105
  91.5 1.0 constant_dynamic-slice_fusion.8
  92.7 1.1 constant_dynamic-slice_fusion.7
  94.2 2.7 %bitcast_dynamic-update-slice_fusion.6 = (bf16[4,8,128,384]{2,3,1,0:T(8,128)(2,1)}, bf16[8,128,384]{1,2,0:T(8,128)(2,1)S(1)}) fusion(bf16[4,8,128,384]{2,3,1,0:T(8,128)(2,1)} %get-tuple-element.390, s32[]{:T(128)} %get-tuple-element.388, f32[8,128]{1,0:T(8,128)S(1)} %bitcast.236, bf16[4,128,8,128]{1,3,2,0:T(8,128)(2,1)} %get-tuple-element.402, ...), kind=kOutput, calls=%fused_computation.10.clone.1.clone | convolution fusion | flops 102629376 | bytes 2725376 | tf_op jit(solution)/shard_map/while/body/eval_jaxpr/rgd,ld->grl/dot_general | solution.py:101
  97.0 1.2 fusion.105
  99.2 1.0 constant_dynamic-slice_fusion.8
  100.3 1.1 constant_dynamic-slice_fusion.7
  101.9 2.7 %bitcast_dynamic-update-slice_fusion.6 = (bf16[4,8,128,384]{2,3,1,0:T(8,128)(2,1)}, bf16[8,128,384]{1,2,0:T(8,128)(2,1)S(1)}) fusion(bf16[4,8,128,384]{2,3,1,0:T(8,128)(2,1)} %get-tuple-element.390, s32[]{:T(128)} %get-tuple-element.388, f32[8,128]{1,0:T(8,128)S(1)} %bitcast.236, bf16[4,128,8,128]{1,3,2,0:T(8,128)(2,1)} %get-tuple-element.402, ...), kind=kOutput, calls=%fused_computation.10.clone.1.clone | convolution fusion | flops 102629376 | bytes 2725376 | tf_op jit(solution)/shard_map/while/body/eval_jaxpr/rgd,ld->grl/dot_general | solution.py:101
  104.6 1.2 fusion.105
  106.8 1.0 constant_dynamic-slice_fusion.8
  107.9 1.1 constant_dynamic-slice_fusion.7
  109.5 2.7 %bitcast_dynamic-update-slice_fusion.6 = (bf16[4,8,128,384]{2,3,1,0:T(8,128)(2,1)}, bf16[8,128,384]{1,2,0:T(8,128)(2,1)S(1)}) fusion(bf16[4,8,128,384]{2,3,1,0:T(8,128)(2,1)} %get-tuple-element.390, s32[]{:T(128)} %get-tuple-element.388, f32[8,128]{1,0:T(8,128)S(1)} %bitcast.236, bf16[4,128,8,128]{1,3,2,0:T(8,128)(2,1)} %get-tuple-element.402, ...), kind=kOutput, calls=%fused_computation.10.clone.1.clone | convolution fusion | flops 102629376 | bytes 2725376 | tf_op jit(solution)/shard_map/while/body/eval_jaxpr/rgd,ld->grl/dot_general | solution.py:101
  112.2 1.2 fusion.105
  114.4 3.2 %fusion.71 = f32[4,384,128,1]{1,2,3,0:T(8,128)S(1)} fusion(bf16[4,8,128,384]{2,3,1,0:T(8,128)(2,1)} %get-tuple-element.407, bf16[4,128,8,128]{1,3,2,0:T(8,128)(2,1)} %copy-done.4), kind=kOutput, calls=%fused_computation.93 | convolution fusion | flops 402653184 | bytes 4980736 | tf_op jit(solution)/shard_map/hgrl,hrgd->lhd/dot_general | solution.py:115
  119.1 1.1 pad_maximum_fusion
  120.6 1.3 copy.70
  122.7 22.6 %reduce-scatter.2.cloned.1.call-done = f32[64,1024]{1,0:T(8,128)} async-done(((f32[256,1024]{1,0:T(8,128)}), f32[64,1024]{1,0:T(8,128)}) %reduce-scatter.2.cloned.1.call-update) | async-done | bytes 262160 | tf_op jit(solution)/shard_map/reduce_scatter | solution.py:124
  145.3 1.6 %convert_bitcast_fusion = bf16[1,64,1024]{2,1,0:T(8,128)(2,1)} fusion(f32[64,1024]{1,0:T(8,128)} %reduce-scatter.2.cloned.1.call-done), kind=kLoop, calls=%fused_computation.62 | loop fusion | flops 65536 | bytes 393216 | tf_op jit(solution)/shard_map/broadcast_in_dim | solution.py:129
  (109 shorter events, 22.1 us)
Async XLA Ops:
  7.2 54.6 %copy-start = (f32[1,1,128]{2,1,0:T(1,128)S(1)}, f32[1,1,128]{2,1,0:T(1,128)}, u32[]{:S(2)}) copy-start(f32[1,1,128]{2,1,0:T(1,128)} %param.19) | copy-start | bytes 1540
  7.2 23.4 %copy-start.12 = (bf16[1,1,128,1024]{3,2,1,0:T(8,128)(2,1)S(1)}, bf16[1,1,128,1024]{3,2,1,0:T(8,128)(2,1)}, u32[]{:S(2)}) copy-start(bf16[1,1,128,1024]{3,2,1,0:T(8,128)(2,1)} %param.16) | copy-start | bytes 786436
  7.2 23.5 %copy-start.11 = (bf16[1,1,128,4096]{3,2,1,0:T(8,128)(2,1)S(1)}, bf16[1,1,128,4096]{3,2,1,0:T(8,128)(2,1)}, u32[]{:S(2)}) copy-start(bf16[1,1,128,4096]{3,2,1,0:T(8,128)(2,1)} %param.14) | copy-start | bytes 3145732
  10.5 8.2 %copy-start.15 = (s32[1024]{0:T(1024)}, s32[1024]{0:T(1024)S(1)}, u32[]{:S(2)}) copy-start(s32[1024]{0:T(1024)S(1)} %pad_clamp_fusion) | copy-start | bytes 12292
  12.4 52.6 %all-to-all-start = ((s32[8,1,16]{2,1,0:T(1,128)}), s32[8,1,16]{2,1,0:T(1,128)S(1)}, u32[]{:S(2)}, u32[]{:S(2)}) async-start(s32[8,1,16]{2,1,0:T(1,128)} %bitcast.29), calls=%async_computation | async-start | bytes 8192 | tf_op jit(solution)/shard_map/all_to_all | solution.py:49
  32.9 2.4 %copy-start.10 = (bf16[384,512]{0,1:T(8,128)(2,1)S(1)}, bf16[384,512]{0,1:T(8,128)(2,1)}, u32[]{:S(2)}) copy-start(bf16[384,512]{0,1:T(8,128)(2,1)} %get-tuple-element.194) | copy-start | bytes 1179652
  35.3 0.5 copy-start.13
  37.5 1.7 %copy-start.14 = (pred[384]{0:T(512)(128)(4,1)S(1)}, pred[384]{0:T(512)(128)(4,1)}, u32[]{:S(2)}) copy-start(pred[384]{0:T(512)(128)(4,1)} %copy-done.13) | copy-start | bytes 1156 | tf_op jit(solution)/shard_map/while
  39.2 0.5 copy-start.13
  41.4 1.8 %copy-start.14 = (pred[384]{0:T(512)(128)(4,1)S(1)}, pred[384]{0:T(512)(128)(4,1)}, u32[]{:S(2)}) copy-start(pred[384]{0:T(512)(128)(4,1)} %copy-done.13) | copy-start | bytes 1156 | tf_op jit(solution)/shard_map/while
  43.2 0.5 copy-start.13
  45.3 1.7 %copy-start.14 = (pred[384]{0:T(512)(128)(4,1)S(1)}, pred[384]{0:T(512)(128)(4,1)}, u32[]{:S(2)}) copy-start(pred[384]{0:T(512)(128)(4,1)} %copy-done.13) | copy-start | bytes 1156 | tf_op jit(solution)/shard_map/while
  47.1 0.5 copy-start.13
  49.3 1.8 %copy-start.14 = (pred[384]{0:T(512)(128)(4,1)S(1)}, pred[384]{0:T(512)(128)(4,1)}, u32[]{:S(2)}) copy-start(pred[384]{0:T(512)(128)(4,1)} %copy-done.13) | copy-start | bytes 1156 | tf_op jit(solution)/shard_map/while
  51.0 1.1 copy-start.4
  55.2 2.0 %copy-start.5 = (bf16[1,1,128,4096]{3,2,1,0:T(8,128)(2,1)S(1)}, bf16[1,1,128,4096]{3,2,1,0:T(8,128)(2,1)}, u32[]{:S(2)}) copy-start(bf16[1,1,128,4096]{3,2,1,0:T(8,128)(2,1)} %param.17) | copy-start | bytes 3145732
  59.3 20.3 %copy-start.1 = (bf16[4,8,128,384]{2,3,1,0:T(8,128)(2,1)S(1)}, bf16[4,8,128,384]{2,3,1,0:T(8,128)(2,1)}, u32[]{:S(2)}) copy-start(bf16[4,8,128,384]{2,3,1,0:T(8,128)(2,1)} %get-tuple-element.384) | copy-start | bytes 9437188
  65.1 10.0 %all-to-all-start.1 = ((f32[8,1,16]{2,1,0:T(1,128)}), f32[8,1,16]{2,1,0:T(1,128)S(1)}, u32[]{:S(2)}, u32[]{:S(2)}) async-start(f32[8,1,16]{2,1,0:T(1,128)} %bitcast.32), calls=%async_computation.1 | async-start | bytes 8192 | tf_op jit(solution)/shard_map/all_to_all | solution.py:48
  69.6 75.7 %reduce-scatter.2.cloned.1.call-start = ((), (), s32[]{:S(2)}) async-start(), calls=%async_computation.3 | async-start | bytes 1310720 | tf_op jit(solution)/shard_map/reduce_scatter | solution.py:124
  79.6 2.0 %copy-start.3 = (bf16[4,128,8,128]{1,3,2,0:T(8,128)(2,1)}, bf16[4,128,8,128]{1,3,2,0:T(8,128)(2,1)S(1)}, u32[]{:S(2)}) copy-start(bf16[4,128,8,128]{1,3,2,0:T(8,128)(2,1)S(1)} %fusion.51) | copy-start | bytes 3145732
  86.4 2.9 %copy-start.6 = (bf16[4,128,8,128]{1,3,2,0:T(8,128)(2,1)S(1)}, bf16[4,128,8,128]{1,3,2,0:T(8,128)(2,1)}, u32[]{:S(2)}) copy-start(bf16[4,128,8,128]{1,3,2,0:T(8,128)(2,1)} %get-tuple-element.389) | copy-start | bytes 3145732 | tf_op jit(solution)/shard_map/while
  86.6 4.9 %copy-start.2 = (bf16[4,8,128,384]{2,3,1,0:T(8,128)(2,1)S(1)}, bf16[4,8,128,384]{2,3,1,0:T(8,128)(2,1)}, u32[]{:S(2)}) copy-start(bf16[4,8,128,384]{2,3,1,0:T(8,128)(2,1)} %get-tuple-element.413) | copy-start | bytes 9437188 | tf_op jit(solution)/shard_map/while
  90.6 1.0 copy-start.7
  94.0 3.0 %copy-start.6 = (bf16[4,128,8,128]{1,3,2,0:T(8,128)(2,1)S(1)}, bf16[4,128,8,128]{1,3,2,0:T(8,128)(2,1)}, u32[]{:S(2)}) copy-start(bf16[4,128,8,128]{1,3,2,0:T(8,128)(2,1)} %get-tuple-element.389) | copy-start | bytes 3145732 | tf_op jit(solution)/shard_map/while
  94.2 5.0 %copy-start.2 = (bf16[4,8,128,384]{2,3,1,0:T(8,128)(2,1)S(1)}, bf16[4,8,128,384]{2,3,1,0:T(8,128)(2,1)}, u32[]{:S(2)}) copy-start(bf16[4,8,128,384]{2,3,1,0:T(8,128)(2,1)} %get-tuple-element.413) | copy-start | bytes 9437188 | tf_op jit(solution)/shard_map/while
  98.2 1.0 copy-start.7
  101.6 3.0 %copy-start.6 = (bf16[4,128,8,128]{1,3,2,0:T(8,128)(2,1)S(1)}, bf16[4,128,8,128]{1,3,2,0:T(8,128)(2,1)}, u32[]{:S(2)}) copy-start(bf16[4,128,8,128]{1,3,2,0:T(8,128)(2,1)} %get-tuple-element.389) | copy-start | bytes 3145732 | tf_op jit(solution)/shard_map/while
  101.8 4.9 %copy-start.2 = (bf16[4,8,128,384]{2,3,1,0:T(8,128)(2,1)S(1)}, bf16[4,8,128,384]{2,3,1,0:T(8,128)(2,1)}, u32[]{:S(2)}) copy-start(bf16[4,8,128,384]{2,3,1,0:T(8,128)(2,1)} %get-tuple-element.413) | copy-start | bytes 9437188 | tf_op jit(solution)/shard_map/while
  105.8 1.0 copy-start.7
  109.2 3.0 %copy-start.6 = (bf16[4,128,8,128]{1,3,2,0:T(8,128)(2,1)S(1)}, bf16[4,128,8,128]{1,3,2,0:T(8,128)(2,1)}, u32[]{:S(2)}) copy-start(bf16[4,128,8,128]{1,3,2,0:T(8,128)(2,1)} %get-tuple-element.389) | copy-start | bytes 3145732 | tf_op jit(solution)/shard_map/while
  109.5 4.9 %copy-start.2 = (bf16[4,8,128,384]{2,3,1,0:T(8,128)(2,1)S(1)}, bf16[4,8,128,384]{2,3,1,0:T(8,128)(2,1)}, u32[]{:S(2)}) copy-start(bf16[4,8,128,384]{2,3,1,0:T(8,128)(2,1)} %get-tuple-element.413) | copy-start | bytes 9437188 | tf_op jit(solution)/shard_map/while
  113.4 1.0 copy-start.7
  117.6 1.1 copy-start.9
  119.0 1.6 %copy-start.8 = (bf16[4,128,8,128]{1,3,2,0:T(8,128)(2,1)S(1)}, bf16[4,128,8,128]{1,3,2,0:T(8,128)(2,1)}, u32[]{:S(2)}) copy-start(bf16[4,128,8,128]{1,3,2,0:T(8,128)(2,1)} %get-tuple-element.406) | copy-start | bytes 3145732
Sparse Core Ops, SparseCore 0:
  120.3 24.9 reduce-scatter.1
where the time goes:
time: 155 us; the launch traced here: 154 us
  local copies, waits for them, and re-layouts  35.4 us (23%)
  matrix products  30.5 us (20%)
  waiting for transfers between devices  26.3 us (17%)
  other arithmetic  22.7 us (15%)
  between operations  16.2 us (10%)
  blocking collectives  11.5 us (7%)
  starting transfers between devices  10.8 us (7%)
    reduce_scatter x1, waiting for transfers between devices, body(): lax.psum_scatter(kv_grad[:prefix_rows], 'resp', scatter_dimension=0, tile...  22.6 us
    all_gather x1, blocking collectives, body(): prefix_all = lax.all_gather(prefix_kv[0], 'resp', axis=0, tiled=True)  11.5 us
    dot_general x4, matrix products, head_backward(): jnp.einsum('rgd,ld->grl', grad_head, value_head, preferred_element_type=j...  10.9 us
    unnamed x26, local copies, waits for them, and re-layouts  7.72 us
    dot_general x4, matrix products, head_forward(): jnp.einsum('grl,ld->rgd', prob_bf16, value_head, preferred_element_type=j...  6.96 us
    all_to_all x1, starting transfers between devices, body(): lax.all_to_all(sent_slot, 'dp', split_axis=0, concat_axis=0, tiled=True)  6.33 us
    dynamic_slice x8, local copies, waits for them, and re-layouts, body(): lax.map(head_backward, (key_heads, value_heads, prob_all, out_all, grad_h...  5.12 us
    while x40, local copies, waits for them, and re-layouts  4.94 us
  transfers between devices with their start and end apart: 3, of which 2 were waited for; matrix products, arithmetic and copies ran while one was open for 22% of the time, Pallas kernels for 0%

commit v1 on v0

v1 whole, which is shorter than its diff:
```python
import functools
import math

import jax
import jax.numpy as jnp
from jax import lax
from jax.experimental import pallas as pl
from jax.experimental.pallas import tpu as pltpu
from jax.sharding import PartitionSpec as P

QH = 32
KVH = 4
HD = 128
GQ = 8
BLOCK = 128
PAIR = 2

loss_scale = 65536.0
clip_lower = 0.8
clip_upper = 1.28

MESH = pl.DeviceIdType.MESH


def dot(a, b, dims):
    return lax.dot_general(a, b, (dims, ((), ())), preferred_element_type=jnp.float32)


def kernel(
    n_dp,
    n_resp,
    queries_hbm,
    prefix_hbm,
    resp_hbm,
    direction_hbm,
    base_ref,
    rollout_ref,
    destination_ref,
    advantage_ref,
    lengths_ref,
    blocks_ref,
    query_grad_hbm,
    resp_grad_hbm,
    prefix_grad_hbm,
    q_ref,
    d_ref,
    kv_ref,
    prob_ref,
    core_ref,
    bias_ref,
    qg_ref,
    rg_ref,
    pg_ref,
    row_send,
    row_recv,
    part_send,
    part_recv,
    load_sems,
    own_sems,
    prefix_send_sems,
    prefix_recv_sems,
    row_send_sems,
    row_recv_sems,
    part_send_sems,
    part_recv_sems,
    out_sems,
):
    my_dp, my_resp = lax.axis_index("dp"), lax.axis_index("resp")
    tok = q_ref.shape[0]
    shard = prefix_hbm.shape[0]
    total = kv_ref.shape[0]
    prefix_rows = total - tok
    width = GQ * HD
    score_scale = 1.0 / math.sqrt(HD)

    def head_cols(h):
        return pl.ds(pl.multiple_of(h * width, width), width)

    def kv_cols(h, x):
        return pl.ds(pl.multiple_of((x * KVH + h) * HD, HD), HD)

    def load_copies(h):
        return (
            pltpu.make_async_copy(
                queries_hbm.at[:, head_cols(h)], q_ref.at[:, head_cols(h)], load_sems.at[h, 0]
            ),
            pltpu.make_async_copy(
                direction_hbm.at[:, head_cols(h)], d_ref.at[:, head_cols(h)], load_sems.at[h, 1]
            ),
        )

    def shard_rows(owner):
        return pl.ds(pl.multiple_of(owner * shard, shard), shard)

    own_copies = (
        pltpu.make_async_copy(
            resp_hbm, kv_ref.at[pl.ds(prefix_rows, tok), :], own_sems.at[0]
        ),
        pltpu.make_async_copy(prefix_hbm, kv_ref.at[shard_rows(my_resp), :], own_sems.at[1]),
    )

    def resp_peer(k):
        return (my_dp, lax.rem(my_resp + k, n_resp))

    def dp_peer(k):
        return (lax.rem(my_dp + k, n_dp), my_resp)

    def prefix_copy(k, h, x, owner):
        return pltpu.make_async_remote_copy(
            src_ref=prefix_hbm.at[:, kv_cols(h, x)],
            dst_ref=kv_ref.at[shard_rows(owner), kv_cols(h, x)],
            send_sem=prefix_send_sems.at[k - 1, h, x],
            recv_sem=prefix_recv_sems.at[k - 1, h, x],
            device_id=resp_peer(k),
            device_id_type=MESH,
        )

    def row_copy(k):
        return pltpu.make_async_remote_copy(
            src_ref=row_send,
            dst_ref=row_recv.at[k - 1],
            send_sem=row_send_sems.at[k - 1],
            recv_sem=row_recv_sems.at[k - 1],
            device_id=dp_peer(k),
            device_id_type=MESH,
        )

    def part_copy(k, h):
        return pltpu.make_async_remote_copy(
            src_ref=part_send.at[h, lax.rem(my_resp + k, n_resp)],
            dst_ref=part_recv.at[k - 1, h],
            send_sem=part_send_sems.at[k - 1, h],
            recv_sem=part_recv_sems.at[k - 1, h],
            device_id=resp_peer(k),
            device_id_type=MESH,
        )

    barrier = pltpu.get_barrier_semaphore()
    for k in range(1, n_resp):
        pl.semaphore_signal(barrier, inc=1, device_id=resp_peer(k), device_id_type=MESH)
    for k in range(1, n_dp):
        pl.semaphore_signal(barrier, inc=1, device_id=dp_peer(k), device_id_type=MESH)
    for copy in own_copies:
        copy.start()
    for h in range(KVH):
        for copy in load_copies(h):
            copy.start()

    row_send[...] = jnp.zeros_like(row_send)
    row_send[0:1, :] = rollout_ref[...]
    row_send[1:2, :] = destination_ref[...].astype(jnp.float32)
    key_index = lax.broadcasted_iota(jnp.int32, (total, tok), 0)
    query_index = lax.broadcasted_iota(jnp.int32, (total, tok), 1)
    allowed = ((key_index < prefix_rows) & (key_index < blocks_ref[0, 0] * BLOCK)) | (
        (key_index >= prefix_rows) & (key_index - prefix_rows <= query_index)
    )
    bias_ref[...] = jnp.where(allowed, 0.0, -1e30)

    pl.semaphore_wait(barrier, n_resp - 1 + n_dp - 1)
    for h in range(KVH):
        for k in range(1, n_resp):
            for x in range(2):
                prefix_copy(k, h, x, my_resp).start()
    for k in range(1, n_dp):
        row_copy(k).start()
    for copy in own_copies:
        copy.wait()

    def forward(h, gained):
        for copy in load_copies(h):
            copy.wait()
        for k in range(1, n_resp):
            for x in range(2):
                prefix_copy(k, h, x, lax.rem(my_resp + n_resp - k, n_resp)).wait_recv()
        keys = kv_ref[:, kv_cols(h, 0)]
        values = kv_ref[:, kv_cols(h, 1)]
        bias = jnp.concatenate([bias_ref[...]] * PAIR, axis=1)
        for g in range(0, GQ, PAIR):
            starts = [pl.multiple_of(h * width + (g + i) * HD, HD) for i in range(PAIR)]
            q_rows = jnp.concatenate([q_ref[:, pl.ds(s, HD)] for s in starts], axis=0)
            d_rows = jnp.concatenate([d_ref[:, pl.ds(s, HD)] for s in starts], axis=0)
            scores = dot(keys, q_rows, ((1,), (1,))) * (score_scale * math.log2(math.e)) + bias
            shifted = jnp.exp2(scores - jnp.max(scores, axis=0, keepdims=True))
            inverse = 1.0 / jnp.sum(shifted, axis=0, keepdims=True)
            prob = (shifted * inverse).astype(jnp.bfloat16)
            wide = prob.astype(jnp.float32)
            toward = dot(values, d_rows, ((1,), (1,)))
            delta = jnp.sum(wide * toward, axis=0, keepdims=True)
            cols = pl.ds(g * HD, PAIR * HD)
            prob_ref[h, :, cols] = prob
            core_ref[h, :, cols] = (wide * (toward - delta)).astype(jnp.bfloat16)
            for i in range(PAIR):
                gained = gained + delta[:, i * HD : (i + 1) * HD]
        return gained

    gained = lax.fori_loop(0, KVH, forward, jnp.zeros((1, tok), jnp.float32))

    slot = (lax.broadcasted_iota(jnp.int32, (tok, tok), 0) + my_dp * tok).astype(jnp.float32)
    placed = jnp.where(row_send[1:2, :] == slot, row_send[0:1, :], 0.0)
    for k in range(1, n_dp):
        row_copy(k).wait_recv()
        placed = placed + jnp.where(
            row_recv[k - 1, 1:2, :] == slot, row_recv[k - 1, 0:1, :], 0.0
        )
    old = jnp.sum(placed.T, axis=0, keepdims=True)
    ratio = jnp.clip(jnp.exp(base_ref[...] + gained - old), clip_lower, clip_upper)
    length = lengths_ref[0, 0]
    coeff = jnp.where(
        lax.broadcasted_iota(jnp.int32, (1, tok), 1) < length,
        (-loss_scale * ratio) * advantage_ref[0, 0] / length.astype(jnp.float32),
        0.0,
    )
    coeff_rows = jnp.broadcast_to(coeff, (tok, tok)).T

    def kv_backward(h, carry):
        starts = [pl.multiple_of(h * width + g * HD, HD) for g in range(GQ)]
        for x, source, weights, factor in (
            (0, q_ref, core_ref, coeff_rows * score_scale),
            (1, d_ref, prob_ref, coeff_rows),
        ):
            rows = jnp.concatenate(
                [
                    (source[:, pl.ds(s, HD)].astype(jnp.float32) * factor).astype(jnp.bfloat16)
                    for s in starts
                ],
                axis=0,
            )
            grad = dot(weights[h], rows, ((1,), (0,))).astype(jnp.bfloat16)
            for owner in range(n_resp):
                part_send[h, owner, x] = grad[owner * shard : (owner + 1) * shard]
            rg_ref[:, kv_cols(h, x)] = grad[prefix_rows:]
        for k in range(1, n_resp):
            part_copy(k, h).start()
        return carry

    lax.fori_loop(0, KVH, kv_backward, 0)
    resp_out = pltpu.make_async_copy(rg_ref, resp_grad_hbm, out_sems.at[KVH])
    resp_out.start()

    def query_out(h):
        return pltpu.make_async_copy(
            qg_ref.at[:, head_cols(h)], query_grad_hbm.at[:, head_cols(h)], out_sems.at[h]
        )

    def query_backward(h, carry):
        grad = dot(kv_ref[:, kv_cols(h, 0)], core_ref[h], ((0,), (0,)))
        for g in range(GQ):
            one = grad[:, g * HD : (g + 1) * HD] * (coeff * score_scale)
            start = pl.multiple_of(h * width + g * HD, HD)
            qg_ref[:, pl.ds(start, HD)] = one.T.astype(jnp.bfloat16)
        query_out(h).start()
        return carry

    lax.fori_loop(0, KVH, query_backward, 0)

    for h in range(KVH):
        for k in range(1, n_resp):
            part_copy(k, h).wait_recv()
        for x in range(2):
            summed = part_send[h, my_resp, x].astype(jnp.float32)
            for k in range(1, n_resp):
                summed = summed + part_recv[k - 1, h, x].astype(jnp.float32)
            pg_ref[:, kv_cols(h, x)] = summed.astype(jnp.bfloat16)
    prefix_out = pltpu.make_async_copy(pg_ref, prefix_grad_hbm, out_sems.at[KVH + 1])
    prefix_out.start()

    for k in range(1, n_dp):
        row_copy(k).wait_send()
    for h in range(KVH):
        for k in range(1, n_resp):
            for x in range(2):
                prefix_copy(k, h, x, my_resp).wait_send()
            part_copy(k, h).wait_send()
        query_out(h).wait()
    resp_out.wait()
    prefix_out.wait()


def body(
    queries,
    prefix_kv,
    resp_kv,
    direction,
    base_logprob,
    rollout_logprob,
    destination,
    advantage,
    lengths,
    prefix_blocks,
):
    n_dp, n_resp = lax.axis_size("dp"), lax.axis_size("resp")
    tok = queries.shape[2]
    shard, kv_width = prefix_kv.shape[1:]
    total = n_resp * shard + tok
    columns = QH * HD
    any_spec = pl.BlockSpec(memory_space=pl.ANY)
    vmem_spec = pl.BlockSpec(memory_space=pltpu.VMEM)
    smem_spec = pl.BlockSpec(memory_space=pltpu.SMEM)
    dma = pltpu.SemaphoreType.DMA
    bf16, f32 = jnp.bfloat16, jnp.float32
    query_grad, resp_grad, prefix_grad = pl.pallas_call(
        functools.partial(kernel, n_dp, n_resp),
        out_shape=(
            jax.ShapeDtypeStruct((tok, columns), bf16),
            jax.ShapeDtypeStruct((tok, kv_width), bf16),
            jax.ShapeDtypeStruct((shard, kv_width), bf16),
        ),
        in_specs=[any_spec] * 4 + [vmem_spec] * 3 + [smem_spec] * 3,
        out_specs=(any_spec, any_spec, any_spec),
        scratch_shapes=[
            pltpu.VMEM((tok, columns), bf16),
            pltpu.VMEM((tok, columns), bf16),
            pltpu.VMEM((total, kv_width), bf16),
            pltpu.VMEM((KVH, total, GQ * tok), bf16),
            pltpu.VMEM((KVH, total, GQ * tok), bf16),
            pltpu.VMEM((total, tok), f32),
            pltpu.VMEM((tok, columns), bf16),
            pltpu.VMEM((tok, kv_width), bf16),
            pltpu.VMEM((shard, kv_width), bf16),
            pltpu.VMEM((8, tok), f32),
            pltpu.VMEM((n_dp - 1, 8, tok), f32),
            pltpu.VMEM((KVH, n_resp, 2, shard, HD), bf16),
            pltpu.VMEM((n_resp - 1, KVH, 2, shard, HD), bf16),
            dma((KVH, 2)),
            dma((2,)),
            dma((n_resp - 1, KVH, 2)),
            dma((n_resp - 1, KVH, 2)),
            dma((n_dp - 1,)),
            dma((n_dp - 1,)),
            dma((n_resp - 1, KVH)),
            dma((n_resp - 1, KVH)),
            dma((KVH + 2,)),
        ],
        compiler_params=pltpu.CompilerParams(
            collective_id=0, has_side_effects=True, vmem_limit_bytes=56 << 20
        ),
    )(
        queries[0, 0],
        prefix_kv[0],
        resp_kv[0, 0],
        direction[0, 0],
        base_logprob[0],
        rollout_logprob[0],
        destination[0],
        advantage,
        lengths,
        prefix_blocks,
    )
    return query_grad[None, None], resp_grad[None, None], prefix_grad[None]


def solution(mesh):
    return jax.shard_map(
        body,
        mesh=mesh,
        in_specs=(
            P("dp", "resp", None, None),
            P("dp", "resp", None),
            P("dp", "resp", None, None),
            P("dp", "resp", None, None),
            P("dp", "resp", None),
            P("dp", "resp", None),
            P("dp", "resp", None),
            P("dp", "resp"),
            P("dp", "resp"),
            P("dp", "resp"),
        ),
        out_specs=(P("dp", "resp", None, None), P("dp", "resp", None, None), P("dp", "resp", None)),
        check_vma=False,
    )
```

time: 155 us -> 31.9 us (0.21)
  local copies, waits for them, and re-layouts: 35.4 us -> 3.99 us
  matrix products: 30.5 us -> 0 us
  waiting for transfers between devices: 26.3 us -> 0 us
  Pallas kernels: 0 us -> 25.1 us
  other arithmetic: 22.7 us -> 0 us
  between operations: 16.2 us -> 2.59 us
  blocking collectives: 11.5 us -> 0 us
  starting transfers between devices: 10.8 us -> 0 us
    dot_general x14 -> x0, matrix products: 27.9 us -> none  [the longest x4 10.9 us: head_backward(): jnp.einsum('rgd,ld->grl', grad_head, value_head, preferred_element_type=j...]
    pallas_call x0 -> x1, Pallas kernels: none -> 25.1 us  [body(): pl.pallas_call(functools.partial(kernel, n_dp, n_resp), out_shape=(jax.Sh...]
    reduce_scatter x1 -> x0, waiting for transfers between devices: 22.6 us -> none  [body(): lax.psum_scatter(kv_grad[:prefix_rows], 'resp', scatter_dimension=0, tile...]
    all_gather x1 -> x0, blocking collectives: 11.5 us -> none  [body(): prefix_all = lax.all_gather(prefix_kv[0], 'resp', axis=0, tiled=True)]
    all_to_all x2 -> x0, starting transfers between devices: 10.8 us -> none  [the longest x1 6.33 us: body(): lax.all_to_all(sent_slot, 'dp', split_axis=0, concat_axis=0, tiled=True)]
    dynamic_slice x16 -> x0, local copies, waits for them, and re-layouts: 9.72 us -> none  [the longest x8 5.12 us: body(): lax.map(head_backward, (key_heads, value_heads, prob_all, out_all, grad_h...]
    while x40 -> x0, local copies, waits for them, and re-layouts: 4.94 us -> none
    another operation x2 -> x0, local copies, waits for them, and re-layouts: 4.79 us -> none
  transfers between devices with their start and end apart: 3 -> 0, of which waited for: 2 -> 0; matrix products, arithmetic and copies ran while one was open for 22% -> 0% of each run, Pallas kernels for 0% -> 0%
where the time goes in v1:
time: 31.9 us; the launch traced here: 31.7 us
  Pallas kernels  25.1 us (79%)
  local copies, waits for them, and re-layouts  3.99 us (13%)
  between operations  2.59 us (8%)
    pallas_call x1, Pallas kernels, body(): pl.pallas_call(functools.partial(kernel, n_dp, n_resp), out_shape=(jax.Sh...  25.1 us
    unnamed x7, local copies, waits for them, and re-layouts  3.99 us

profile of v1, /device:TPU:0, one launch (start us, length us, event | category | flops | bytes accessed | tf_op | source)
XLA Modules:
  0.0 31.7 jit_solution(3342610289570918911)
XLA Ops:
  2.6 25.1 %shard_map.121 = (bf16[128,4096]{1,0:T(8,128)(2,1)}, bf16[128,1024]{1,0:T(8,128)(2,1)}, bf16[64,1024]{1,0:T(8,128)(2,1)}) custom-call(bf16[128,4096]{1,0:T(8,128)(2,1)} %bitcast.11, bf16[64,1024]{1,0:T(8,128)(2,1)} %bitcast.16, bf16[128,1024]{1,0:T(8,128)(2,1)} %bitcast.14, bf16[128,4096]{1,0:T(8,128)(2,1)} %bitcast.12, f32[1,128]{1,0:T(1,128)} %bitcast.17, ...), custom_call_target="tpu_custom_call" | custom-call | tf_op jit(solution)/shard_map/pallas_call | solution.py:301
  27.7 0.0 copy-start
  27.7 2.3 %copy.19 = bf16[1,1,128,4096]{3,2,1,0:T(8,128)(2,1)} copy(bf16[1,1,128,4096]{3,2,1,0:T(8,128)(2,1)} %bitcast.10) | data formatting | bytes 2097152
  30.0 0.0 copy-done
  30.0 0.0 copy-start.1
  30.0 0.7 %copy.20 = bf16[1,1,128,1024]{3,2,1,0:T(8,128)(2,1)} copy(bf16[1,1,128,1024]{3,2,1,0:T(8,128)(2,1)S(1)} %bitcast.13) | data formatting | bytes 524288
  30.7 0.3 copy-done.1
  31.0 0.7 %copy.21 = bf16[1,64,1024]{2,1,0:T(8,128)(2,1)} copy(bf16[1,64,1024]{2,1,0:T(8,128)(2,1)S(1)} %bitcast.15) | data formatting | bytes 262144
Async XLA Ops:
  27.7 2.3 %copy-start = (bf16[128,1024]{1,0:T(8,128)(2,1)S(1)}, bf16[128,1024]{1,0:T(8,128)(2,1)}, u32[]{:S(2)}) copy-start(bf16[128,1024]{1,0:T(8,128)(2,1)} %get-tuple-element.7) | copy-start | bytes 786436
  30.0 1.0 %copy-start.1 = (bf16[64,1024]{1,0:T(8,128)(2,1)S(1)}, bf16[64,1024]{1,0:T(8,128)(2,1)}, u32[]{:S(2)}) copy-start(bf16[64,1024]{1,0:T(8,128)(2,1)} %get-tuple-element.8) | copy-start | bytes 393220

commit v2 on v1

--- a/solution.py
+++ b/solution.py
@@ -33,24 +33,21 @@
     prefix_hbm,
     resp_hbm,
     direction_hbm,
-    base_ref,
-    rollout_ref,
-    destination_ref,
+    base_hbm,
+    rollout_hbm,
+    destination_hbm,
     advantage_ref,
     lengths_ref,
     blocks_ref,
-    query_grad_hbm,
-    resp_grad_hbm,
-    prefix_grad_hbm,
+    qg_ref,
+    rg_ref,
+    pg_ref,
     q_ref,
     d_ref,
     kv_ref,
     prob_ref,
     core_ref,
     bias_ref,
-    qg_ref,
-    rg_ref,
-    pg_ref,
     row_send,
     row_recv,
     part_send,
@@ -63,7 +60,10 @@
     row_recv_sems,
     part_send_sems,
     part_recv_sems,
-    out_sems,
+    base_ref,
+    rollout_ref,
+    destination_ref,
+    small_sems,
 ):
     my_dp, my_resp = lax.axis_index("dp"), lax.axis_index("resp")
     tok = q_ref.shape[0]
@@ -135,34 +135,48 @@
             device_id_type=MESH,
         )
 
+    small_copies = [
+        pltpu.make_async_copy(source, target, small_sems.at[i])
+        for i, (source, target) in enumerate(
+            (
+                (rollout_hbm, rollout_ref),
+                (destination_hbm, destination_ref),
+                (base_hbm, base_ref),
+            )
+        )
+    ]
+
     barrier = pltpu.get_barrier_semaphore()
     for k in range(1, n_resp):
         pl.semaphore_signal(barrier, inc=1, device_id=resp_peer(k), device_id_type=MESH)
     for k in range(1, n_dp):
         pl.semaphore_signal(barrier, inc=1, device_id=dp_peer(k), device_id_type=MESH)
+    for copy in small_copies:
+        copy.start()
     for copy in own_copies:
         copy.start()
     for h in range(KVH):
         for copy in load_copies(h):
             copy.start()
 
+    pl.semaphore_wait(barrier, n_resp - 1 + n_dp - 1)
+    for h in range(KVH):
+        for k in range(1, n_resp):
+            for x in range(2):
+                prefix_copy(k, h, x, my_resp).start()
+    for copy in small_copies:
+        copy.wait()
     row_send[...] = jnp.zeros_like(row_send)
     row_send[0:1, :] = rollout_ref[...]
     row_send[1:2, :] = destination_ref[...].astype(jnp.float32)
+    for k in range(1, n_dp):
+        row_copy(k).start()
     key_index = lax.broadcasted_iota(jnp.int32, (total, tok), 0)
     query_index = lax.broadcasted_iota(jnp.int32, (total, tok), 1)
     allowed = ((key_index < prefix_rows) & (key_index < blocks_ref[0, 0] * BLOCK)) | (
         (key_index >= prefix_rows) & (key_index - prefix_rows <= query_index)
     )
     bias_ref[...] = jnp.where(allowed, 0.0, -1e30)
-
-    pl.semaphore_wait(barrier, n_resp - 1 + n_dp - 1)
-    for h in range(KVH):
-        for k in range(1, n_resp):
-            for x in range(2):
-                prefix_copy(k, h, x, my_resp).start()
-    for k in range(1, n_dp):
-        row_copy(k).start()
     for copy in own_copies:
         copy.wait()
 
@@ -234,13 +248,6 @@
         return carry
 
     lax.fori_loop(0, KVH, kv_backward, 0)
-    resp_out = pltpu.make_async_copy(rg_ref, resp_grad_hbm, out_sems.at[KVH])
-    resp_out.start()
-
-    def query_out(h):
-        return pltpu.make_async_copy(
-            qg_ref.at[:, head_cols(h)], query_grad_hbm.at[:, head_cols(h)], out_sems.at[h]
-        )
 
     def query_backward(h, carry):
         grad = dot(kv_ref[:, kv_cols(h, 0)], core_ref[h], ((0,), (0,)))
@@ -248,7 +255,6 @@
             one = grad[:, g * HD : (g + 1) * HD] * (coeff * score_scale)
             start = pl.multiple_of(h * width + g * HD, HD)
             qg_ref[:, pl.ds(start, HD)] = one.T.astype(jnp.bfloat16)
-        query_out(h).start()
         return carry
 
     lax.fori_loop(0, KVH, query_backward, 0)
@@ -261,8 +267,6 @@
             for k in range(1, n_resp):
                 summed = summed + part_recv[k - 1, h, x].astype(jnp.float32)
             pg_ref[:, kv_cols(h, x)] = summed.astype(jnp.bfloat16)
-    prefix_out = pltpu.make_async_copy(pg_ref, prefix_grad_hbm, out_sems.at[KVH + 1])
-    prefix_out.start()
 
     for k in range(1, n_dp):
         row_copy(k).wait_send()
@@ -271,9 +275,18 @@
             for x in range(2):
                 prefix_copy(k, h, x, my_resp).wait_send()
             part_copy(k, h).wait_send()
-        query_out(h).wait()
-    resp_out.wait()
-    prefix_out.wait()
+
+
+def deliver(*refs):
+    count = len(refs) // 2
+    sems = refs[-1]
+    copies = [
+        pltpu.make_async_copy(refs[i], refs[count + i], sems.at[i]) for i in range(count)
+    ]
+    for copy in copies:
+        copy.start()
+    for copy in copies:
+        copy.wait()
 
 
 def body(
@@ -298,15 +311,15 @@
     smem_spec = pl.BlockSpec(memory_space=pltpu.SMEM)
     dma = pltpu.SemaphoreType.DMA
     bf16, f32 = jnp.bfloat16, jnp.float32
-    query_grad, resp_grad, prefix_grad = pl.pallas_call(
+    grads = pl.pallas_call(
         functools.partial(kernel, n_dp, n_resp),
         out_shape=(
-            jax.ShapeDtypeStruct((tok, columns), bf16),
-            jax.ShapeDtypeStruct((tok, kv_width), bf16),
-            jax.ShapeDtypeStruct((shard, kv_width), bf16),
+            pltpu.VMEM((tok, columns), bf16),
+            pltpu.VMEM((tok, kv_width), bf16),
+            pltpu.VMEM((shard, kv_width), bf16),
         ),
-        in_specs=[any_spec] * 4 + [vmem_spec] * 3 + [smem_spec] * 3,
-        out_specs=(any_spec, any_spec, any_spec),
+        in_specs=[any_spec] * 7 + [smem_spec] * 3,
+        out_specs=(vmem_spec, vmem_spec, vmem_spec),
         scratch_shapes=[
             pltpu.VMEM((tok, columns), bf16),
             pltpu.VMEM((tok, columns), bf16),
@@ -314,9 +327,6 @@
             pltpu.VMEM((KVH, total, GQ * tok), bf16),
             pltpu.VMEM((KVH, total, GQ * tok), bf16),
             pltpu.VMEM((total, tok), f32),
-            pltpu.VMEM((tok, columns), bf16),
-            pltpu.VMEM((tok, kv_width), bf16),
-            pltpu.VMEM((shard, kv_width), bf16),
             pltpu.VMEM((8, tok), f32),
             pltpu.VMEM((n_dp - 1, 8, tok), f32),
             pltpu.VMEM((KVH, n_resp, 2, shard, HD), bf16),
@@ -329,7 +339,10 @@
             dma((n_dp - 1,)),
             dma((n_resp - 1, KVH)),
             dma((n_resp - 1, KVH)),
-            dma((KVH + 2,)),
+            pltpu.VMEM((1, tok), f32),
+            pltpu.VMEM((1, tok), f32),
+            pltpu.VMEM((1, tok), jnp.int32),
+            dma((3,)),
         ],
         compiler_params=pltpu.CompilerParams(
             collective_id=0, has_side_effects=True, vmem_limit_bytes=56 << 20
@@ -346,6 +359,13 @@
         lengths,
         prefix_blocks,
     )
+    query_grad, resp_grad, prefix_grad = pl.pallas_call(
+        deliver,
+        out_shape=tuple(jax.ShapeDtypeStruct(g.shape, g.dtype) for g in grads),
+        in_specs=[vmem_spec] * 3,
+        out_specs=(any_spec, any_spec, any_spec),
+        scratch_shapes=[dma((3,))],
+    )(*[pltpu.with_memory_space_constraint(g, pltpu.VMEM) for g in grads])
     return query_grad[None, None], resp_grad[None, None], prefix_grad[None]
 
 

time: 31.9 us -> 27.7 us (0.87)
  local copies, waits for them, and re-layouts: 3.99 us -> 0 us
    unnamed x7 -> x0, local copies, waits for them, and re-layouts: 3.99 us -> none
    pallas_call x1 -> x2, Pallas kernels: 25.1 us -> 25 us  [the longest x1 23.8 us: body(): pl.pallas_call(functools.partial(kernel, n_dp, n_resp), out_shape=(pltpu....]
where the time goes in v2:
time: 27.7 us; the launch traced here: 27.5 us
  Pallas kernels  25 us (90%)
  between operations  2.58 us (9%)
    pallas_call x1, Pallas kernels, body(): pl.pallas_call(functools.partial(kernel, n_dp, n_resp), out_shape=(pltpu....  23.8 us
    pallas_call x1, Pallas kernels, body(): pl.pallas_call(deliver, out_shape=tuple((jax.ShapeDtypeStruct(g.shape, g....  1.12 us

profile of v2, /device:TPU:0, one launch (start us, length us, event | category | flops | bytes accessed | tf_op | source)
XLA Modules:
  0.0 27.5 jit_solution(7766305459562269598)
XLA Ops:
  2.6 23.8 %shard_map.121 = (bf16[128,4096]{1,0:T(8,128)(2,1)S(1)}, bf16[128,1024]{1,0:T(8,128)(2,1)S(1)}, bf16[64,1024]{1,0:T(8,128)(2,1)S(1)}) custom-call(bf16[128,4096]{1,0:T(8,128)(2,1)} %bitcast.10, bf16[64,1024]{1,0:T(8,128)(2,1)} %bitcast.13, bf16[128,1024]{1,0:T(8,128)(2,1)} %bitcast.12, bf16[128,4096]{1,0:T(8,128)(2,1)} %bitcast.11, f32[1,128]{1,0:T(1,128)} %bitcast.14, ...), custom_call_target="tpu_custom_call" | custom-call | tf_op jit(solution)/shard_map/pallas_call | solution.py:314
  26.4 1.1 %shard_map.122 = (bf16[128,4096]{1,0:T(8,128)(2,1)}, bf16[128,1024]{1,0:T(8,128)(2,1)}, bf16[64,1024]{1,0:T(8,128)(2,1)}) custom-call(bf16[128,4096]{1,0:T(8,128)(2,1)S(1)} %get-tuple-element.9.refs_0_, bf16[128,1024]{1,0:T(8,128)(2,1)S(1)} %get-tuple-element.10.refs_1_, bf16[64,1024]{1,0:T(8,128)(2,1)S(1)} %get-tuple-element.11.refs_2_), custom_call_target="tpu_custom_call" | custom-call | tf_op jit(solution)/shard_map/pallas_call | solution.py:362

commit v3 on v2

--- a/solution.py
+++ b/solution.py
@@ -13,7 +13,7 @@
 HD = 128
 GQ = 8
 BLOCK = 128
-PAIR = 2
+PAIR = 4
 
 loss_scale = 65536.0
 clip_lower = 0.8
@@ -64,6 +64,7 @@
     rollout_ref,
     destination_ref,
     small_sems,
+    rows_ref,
 ):
     my_dp, my_resp = lax.axis_index("dp"), lax.axis_index("resp")
     tok = q_ref.shape[0]
@@ -239,10 +240,10 @@
                 ],
                 axis=0,
             )
-            grad = dot(weights[h], rows, ((1,), (0,))).astype(jnp.bfloat16)
+            rows_ref[h, x] = rows
+            grad = dot(weights[h, :prefix_rows], rows, ((1,), (0,))).astype(jnp.bfloat16)
             for owner in range(n_resp):
                 part_send[h, owner, x] = grad[owner * shard : (owner + 1) * shard]
-            rg_ref[:, kv_cols(h, x)] = grad[prefix_rows:]
         for k in range(1, n_resp):
             part_copy(k, h).start()
         return carry
@@ -255,6 +256,9 @@
             one = grad[:, g * HD : (g + 1) * HD] * (coeff * score_scale)
             start = pl.multiple_of(h * width + g * HD, HD)
             qg_ref[:, pl.ds(start, HD)] = one.T.astype(jnp.bfloat16)
+        for x, weights in ((0, core_ref), (1, prob_ref)):
+            own = dot(weights[h, prefix_rows:], rows_ref[h, x], ((1,), (0,)))
+            rg_ref[:, kv_cols(h, x)] = own.astype(jnp.bfloat16)
         return carry
 
     lax.fori_loop(0, KVH, query_backward, 0)
@@ -343,6 +347,7 @@
             pltpu.VMEM((1, tok), f32),
             pltpu.VMEM((1, tok), jnp.int32),
             dma((3,)),
+            pltpu.VMEM((KVH, 2, GQ * tok, HD), bf16),
         ],
         compiler_params=pltpu.CompilerParams(
             collective_id=0, has_side_effects=True, vmem_limit_bytes=56 << 20

time: 27.7 us -> 27.6 us (level)
  no operation moved by 1% of the time
where the time goes in v3:
time: 27.6 us; the launch traced here: 27.4 us
  Pallas kernels  24.8 us (90%)
  between operations  2.58 us (9%)
    pallas_call x1, Pallas kernels, body(): pl.pallas_call(functools.partial(kernel, n_dp, n_resp), out_shape=(pltpu....  23.7 us
    pallas_call x1, Pallas kernels, body(): pl.pallas_call(deliver, out_shape=tuple((jax.ShapeDtypeStruct(g.shape, g....  1.12 us

profile of v3, /device:TPU:0, one launch (start us, length us, event | category | flops | bytes accessed | tf_op | source)
XLA Modules:
  0.0 27.4 jit_solution(9522734887446922371)
XLA Ops:
  2.6 23.7 %shard_map.121 = (bf16[128,4096]{1,0:T(8,128)(2,1)S(1)}, bf16[128,1024]{1,0:T(8,128)(2,1)S(1)}, bf16[64,1024]{1,0:T(8,128)(2,1)S(1)}) custom-call(bf16[128,4096]{1,0:T(8,128)(2,1)} %bitcast.10, bf16[64,1024]{1,0:T(8,128)(2,1)} %bitcast.13, bf16[128,1024]{1,0:T(8,128)(2,1)} %bitcast.12, bf16[128,4096]{1,0:T(8,128)(2,1)} %bitcast.11, f32[1,128]{1,0:T(1,128)} %bitcast.14, ...), custom_call_target="tpu_custom_call" | custom-call | tf_op jit(solution)/shard_map/pallas_call | solution.py:318
  26.3 1.1 %shard_map.122 = (bf16[128,4096]{1,0:T(8,128)(2,1)}, bf16[128,1024]{1,0:T(8,128)(2,1)}, bf16[64,1024]{1,0:T(8,128)(2,1)}) custom-call(bf16[128,4096]{1,0:T(8,128)(2,1)S(1)} %get-tuple-element.9.refs_0_, bf16[128,1024]{1,0:T(8,128)(2,1)S(1)} %get-tuple-element.10.refs_1_, bf16[64,1024]{1,0:T(8,128)(2,1)S(1)} %get-tuple-element.11.refs_2_), custom_call_target="tpu_custom_call" | custom-call | tf_op jit(solution)/shard_map/pallas_call | solution.py:367
